TPU v7x, 32 devices: a whole 2x2x4 slice. The times are simulated.
32 devices in a mesh: row: 8 (over z, core), loop: 4 (over y, x).
Axes of the slice: x: 2, y: 2, z: 4, core: 2. Of those that a mesh axis runs over, the one named last changes fastest.
Arguments:
- student_image: bfloat16 [5120, 1024], P(('row', 'loop')), may hold values from -12 to 12
- student_text: bfloat16 [5120, 1024], P(('row', 'loop')), may hold values from -12 to 12
- teacher_image: bfloat16 [5120, 1024], P('row', 'loop'), may hold values from -12 to 12
- teacher_text: bfloat16 [5120, 1024], P('row', 'loop'), may hold values from -12 to 12
- student_scale: float32 [1], replicated, may hold values from 30 to 100
- teacher_scale: float32 [1], replicated, may hold values from 30 to 100
Outputs:
- loss: float32 [1], replicated
- grad_image: bfloat16 [5120, 1024], P(('row', 'loop'))
- grad_text: bfloat16 [5120, 1024], P(('row', 'loop'))
All inputs are finite; a program needn't handle non-finite values.
Results may differ from a plain program's by a relative error of at most 0.014.
The roundings to bfloat16 on the way count: a program that leaves them out, or rounds other values in their place, can miss the bound.
Values may be sent and summed in bfloat16 or wider, within the bound.
A program may use at most 128 MiB of HBM per device.

v0:
```python
import jax
import jax.numpy as jnp
from jax import lax
from jax.sharding import PartitionSpec as P

EPS = 1e-06


def unit_rows(codes):
    values = codes.astype(jnp.float32)
    norms = jnp.sqrt(jnp.sum(values * values, axis=1, keepdims=True) + EPS)
    return (values / norms, norms)


def back_norm(grad_unit, units, norms):
    inner = jnp.sum(grad_unit * units, axis=1, keepdims=True)
    return ((grad_unit - units * inner) / norms).astype(jnp.bfloat16)


def on_device(
    student_image, student_text, teacher_image, teacher_text, student_scale, teacher_scale
):
    simg_unit, simg_norm = unit_rows(student_image)
    stxt_unit, stxt_norm = unit_rows(student_text)
    simg_own = simg_unit.astype(jnp.bfloat16)
    stxt_own = stxt_unit.astype(jnp.bfloat16)
    timg_full = lax.all_gather(teacher_image, "loop", axis=1, tiled=True)
    timg = unit_rows(timg_full)[0].astype(jnp.bfloat16)
    ttxt_full = lax.all_to_all(teacher_text, "loop", split_axis=0, concat_axis=1, tiled=True)
    ttxt_own = unit_rows(ttxt_full)[0].astype(jnp.bfloat16)
    simg = lax.all_gather(simg_own, "loop", axis=0, tiled=True)
    stxt, ttxt = (
        lax.all_gather(stxt_own, "row", axis=0, tiled=True),
        lax.all_gather(ttxt_own, "row", axis=0, tiled=True),
    )
    sscale = student_scale[0]
    tscale = teacher_scale[0]
    slog = sscale * jnp.einsum("re,ce->rc", simg, stxt, preferred_element_type=jnp.float32)
    tlog = tscale * jnp.einsum("re,ce->rc", timg, ttxt, preferred_element_type=jnp.float32)
    smax, tmax = lax.pmax((jnp.max(slog, axis=1), jnp.max(tlog, axis=1)), "loop")
    sexp = jnp.exp(slog - smax[:, None])
    texp = jnp.exp(tlog - tmax[:, None])
    ssum, tsum, cross = lax.psum(
        (jnp.sum(sexp, axis=1), jnp.sum(texp, axis=1), jnp.sum(texp * (tlog - slog), axis=1)),
        "loop",
    )
    lses = smax + jnp.log(ssum)
    lset = tmax + jnp.log(tsum)
    diverge = cross / tsum - lset + lses
    group_total = lax.psum(jnp.sum(diverge), "row")
    batch_total = simg.shape[0] * lax.axis_size("row")
    loss = (group_total / batch_total).reshape(1)
    probs = jnp.exp(slog - lses[:, None])
    probt = jnp.exp(tlog - lset[:, None])
    grad_logits = (sscale * (probs - probt)).astype(jnp.bfloat16)
    dimg = lax.psum_scatter(
        jnp.dot(grad_logits, stxt, preferred_element_type=jnp.float32).astype(jnp.bfloat16),
        "loop",
        scatter_dimension=0,
        tiled=True,
    ).astype(jnp.float32)
    dtxt = lax.psum_scatter(
        jnp.einsum("rc,re->ce", grad_logits, simg, preferred_element_type=jnp.float32).astype(
            jnp.bfloat16
        ),
        "row",
        scatter_dimension=0,
        tiled=True,
    ).astype(jnp.float32)
    return (loss, back_norm(dimg, simg_unit, simg_norm), back_norm(dtxt, stxt_unit, stxt_norm))


def solution(mesh):
    return jax.shard_map(
        on_device,
        mesh=mesh,
        in_specs=(
            P(("row", "loop"), None),
            P(("row", "loop"), None),
            P("row", "loop"),
            P("row", "loop"),
            P(),
            P(),
        ),
        out_specs=(P(), P(("row", "loop"), None), P(("row", "loop"), None)),
        check_vma=False,
    )
```

profile of v0, /device:TPU:0, one launch (start us, length us, event | category | flops | bytes accessed | tf_op | source)
XLA Modules:
  0.0 265.1 jit_solution(4238910627074843657)
XLA Ops:
  9.1 1.8 fusion.14
  12.1 1.8 fusion.15
  14.0 14.7 %all_to_all.13 = bf16[4,160,256]{2,1,0:T(8,128)(2,1)S(1)} all-to-all(bf16[4,160,256]{2,1,0:T(8,128)(2,1)S(1)} %bitcast.19), channel_id=1, replica_groups=mesh['row'=8,'loop'=4] {'loop'}, dimensions={0} | all-to-all | bytes 655360 | tf_op jit(solution)/shard_map/all_to_all | solution.py:29
  31.2 12.3 %all-gather.5.cloned.1.call-done = bf16[640,1024]{1,0:T(8,128)(2,1)} async-done(((bf16[640,256]{1,0:T(8,128)(2,1)}), bf16[640,1024]{1,0:T(8,128)(2,1)}) %all-gather.5.cloned.1.call-update) | async-done | bytes 1310736 | tf_op jit(solution)/shard_map/all_gather | solution.py:27
  43.5 1.6 fusion.1
  45.2 29.5 %all-gather.9.cloned.1.call-done = bf16[640,1024]{1,0:T(8,128)(2,1)} async-done(((bf16[160,1024]{1,0:T(8,128)(2,1)}), bf16[640,1024]{1,0:T(8,128)(2,1)}) %all-gather.9.cloned.1.call-update) | async-done | bytes 1310736 | tf_op jit(solution)/shard_map/all_gather | solution.py:31
  74.6 35.4 %all-gather.11.cloned.1.call-done = bf16[1280,1024]{1,0:T(8,128)(2,1)} async-done(((bf16[160,1024]{1,0:T(8,128)(2,1)}), bf16[1280,1024]{1,0:T(8,128)(2,1)}) %all-gather.11.cloned.1.call-update) | async-done | bytes 2621456 | tf_op jit(solution)/shard_map/all_gather | solution.py:33
  110.0 4.2 %fusion.16 = (f32[640]{0:T(1024)S(1)}, f32[640,1280]{1,0:T(8,128)S(1)}) fusion(bf16[640,1024]{1,0:T(8,128)(2,1)} %all-gather.9.cloned.1.call-done, bf16[1280,1024]{1,0:T(8,128)(2,1)} %all-gather.11.cloned.1.call-done, f32[]{:T(128)} %bitcast.15), kind=kOutput, calls=%fused_computation.43 | convolution fusion | flops 1679359360 | bytes 7211524 | tf_op jit(solution)/shard_map/re,ce->rc/dot_general | solution.py:38
  114.2 30.8 %all-gather.7.cloned.1.call-done = bf16[1280,1024]{1,0:T(8,128)(2,1)} async-done(((bf16[160,1024]{1,0:T(8,128)(2,1)}), bf16[1280,1024]{1,0:T(8,128)(2,1)}) %all-gather.7.cloned.1.call-update) | async-done | bytes 2621456 | tf_op jit(solution)/shard_map/all_gather | solution.py:34
  144.9 5.8 %fusion.17 = (f32[640]{0:T(1024)S(1)}, f32[640,1280]{1,0:T(8,128)}) fusion(bf16[1280,1024]{1,0:T(8,128)(2,1)} %all-gather.7.cloned.1.call-done, bf16[640,1024]{1,0:T(8,128)(2,1)} %all-gather.5.cloned.1.call-done, f32[640]{0:T(1024)S(1)} %add_sqrt_fusion, f32[]{:T(128)} %bitcast.17), kind=kOutput, calls=%fused_computation.44 | convolution fusion | flops 1681325440 | bytes 7214084 | tf_op jit(solution)/shard_map/re,ce->rc/dot_general | solution.py:39
  150.7 10.0 %all-reduce.1 = (f32[640]{0:T(1024)S(1)}, f32[640]{0:T(1024)S(1)}) all-reduce(f32[640]{0:T(1024)S(1)} %get-tuple-element.14, f32[640]{0:T(1024)S(1)} %get-tuple-element.16), channel_id=1, replica_groups=mesh['row'=8,'loop'=4] {'loop'}, use_global_device_ids=true, to_apply=%region_11.0 | all-reduce | flops 1280 | bytes 10240 | tf_op jit(solution)/shard_map/pmax | solution.py:40
  160.7 3.3 %multiply_reduce_fusion = (f32[640]{0:T(1024)S(1)}, f32[640]{0:T(1024)S(1)}, f32[640]{0:T(1024)S(1)}) fusion(f32[640,1280]{1,0:T(8,128)} %get-tuple-element.17, f32[640,1280]{1,0:T(8,128)S(1)} %get-tuple-element.15, f32[640]{0:T(1024)S(1)} %get-tuple-element.10, f32[640]{0:T(1024)S(1)} %get-tuple-element.9), kind=kLoop, calls=%fused_computation.5 | loop fusion | flops 5732480 | bytes 6566400 | tf_op jit(solution)/shard_map/reduce_sum | solution.py:44
  164.0 14.0 %all-reduce = (f32[640]{0:T(1024)S(1)}, f32[640]{0:T(1024)S(1)}, f32[640]{0:T(1024)S(1)}) all-reduce(f32[640]{0:T(1024)S(1)} %get-tuple-element.5, f32[640]{0:T(1024)S(1)} %get-tuple-element.4, f32[640]{0:T(1024)S(1)} %get-tuple-element.3), channel_id=1, replica_groups=mesh['row'=8,'loop'=4] {'loop'}, use_global_device_ids=true, to_apply=%region_13.0 | all-reduce | flops 1920 | bytes 15360 | tf_op jit(solution)/shard_map/psum | solution.py:43
  178.7 3.0 %multiply_convert_fusion = bf16[640,1280]{1,0:T(8,128)(2,1)S(1)} fusion(f32[640,1280]{1,0:T(8,128)} %get-tuple-element.17, f32[640,1280]{1,0:T(8,128)S(1)} %get-tuple-element.15, f32[640]{0:T(1024)S(1)} %get-tuple-element.12, f32[640]{0:T(1024)S(1)} %get-tuple-element.13, f32[]{:T(128)} %bitcast.16), kind=kLoop, calls=%fused_computation.3 | loop fusion | flops 4096000 | bytes 8197124 | tf_op jit(solution)/shard_map/convert_element_type | solution.py:55
  181.7 1.2 copy-done.2
  182.9 3.0 %convolution_convert_fusion.1 = bf16[640,1024]{1,0:T(8,128)(2,1)} fusion(bf16[640,1280]{1,0:T(8,128)(2,1)S(1)} %multiply_convert_fusion, bf16[1280,1024]{1,0:T(8,128)(2,1)S(1)} %copy-done.4), kind=kOutput, calls=%fused_computation.12 | convolution fusion | flops 1678376960 | bytes 5570560 | tf_op jit(solution)/shard_map/dot_general | solution.py:57
  186.0 5.2 %convolution_convert_fusion = bf16[1280,1024]{1,0:T(8,128)(2,1)} fusion(bf16[640,1280]{1,0:T(8,128)(2,1)} %copy-done.2, bf16[640,1024]{1,0:T(8,128)(2,1)S(1)} %copy-done.5), kind=kOutput, calls=%fused_computation | convolution fusion | flops 1679032320 | bytes 5570560 | tf_op jit(solution)/shard_map/rc,re->ce/dot_general | solution.py:63
  191.2 14.2 %psum.31 = f32[]{:T(128)} all-reduce(f32[]{:T(128)} %get-tuple-element.11), channel_id=1, replica_groups=mesh['row'=8,'loop'=4] {'row'}, use_global_device_ids=true, to_apply=%region_15.0 | all-reduce | flops 1 | bytes 8 | tf_op jit(solution)/shard_map/psum | solution.py:50
  206.1 7.7 %reduce-scatter.3.cloned.1.call-done = bf16[160,1024]{1,0:T(8,128)(2,1)} async-done(((bf16[640,1024]{1,0:T(8,128)(2,1)}), bf16[160,1024]{1,0:T(8,128)(2,1)}) %reduce-scatter.3.cloned.1.call-update) | async-done | bytes 327696 | tf_op jit(solution)/shard_map/reduce_scatter | solution.py:56
  213.8 1.2 fusion.7
  215.0 2.0 fusion.9
  217.0 37.0 %reduce-scatter.5.cloned.1.call-done = bf16[160,1024]{1,0:T(8,128)(2,1)} async-done(((bf16[1280,1024]{1,0:T(8,128)(2,1)}), bf16[160,1024]{1,0:T(8,128)(2,1)}) %reduce-scatter.5.cloned.1.call-update) | async-done | bytes 327696 | tf_op jit(solution)/shard_map/reduce_scatter | solution.py:62
  253.9 1.2 fusion.10
  255.2 2.0 fusion.12
  (34 shorter events, 5.0 us)
Async XLA Ops:
  7.2 6.9 %copy-start.3 = (bf16[640,256]{1,0:T(8,128)(2,1)S(1)}, bf16[640,256]{1,0:T(8,128)(2,1)}, u32[]{:S(2)}) copy-start(bf16[640,256]{1,0:T(8,128)(2,1)} %param.9) | copy-start | bytes 983044
  7.2 36.3 %all-gather.5.cloned.1.call-start = ((), (), s32[]{:S(2)}) async-start(), calls=%async_computation.3 | async-start | bytes 1638400 | tf_op jit(solution)/shard_map/all_gather | solution.py:27
  7.9 66.7 %all-gather.9.cloned.1.call-start = ((), (), s32[]{:S(2)}) async-start(), calls=%async_computation.5 | async-start | bytes 1638400 | tf_op jit(solution)/shard_map/all_gather | solution.py:31
  10.9 99.1 %all-gather.11.cloned.1.call-start = ((), (), s32[]{:S(2)}) async-start(), calls=%async_computation.6 | async-start | bytes 2949120 | tf_op jit(solution)/shard_map/all_gather | solution.py:33
  14.0 131.0 %all-gather.7.cloned.1.call-start = ((), (), s32[]{:S(2)}) async-start(), calls=%async_computation.4 | async-start | bytes 2949120 | tf_op jit(solution)/shard_map/all_gather | solution.py:34
  29.9 183.9 %reduce-scatter.3.cloned.1.call-start = ((), (), s32[]{:S(2)}) async-start(), calls=%async_computation.7 | async-start | bytes 1638400 | tf_op jit(solution)/shard_map/reduce_scatter | solution.py:56
  178.7 4.2 %copy-start.4 = (bf16[1280,1024]{1,0:T(8,128)(2,1)S(1)}, bf16[1280,1024]{1,0:T(8,128)(2,1)}, u32[]{:S(2)}) copy-start(bf16[1280,1024]{1,0:T(8,128)(2,1)} %all-gather.11.cloned.1.call-done) | copy-start | bytes 7864324
  181.7 1.2 copy-start.2
  182.9 3.1 %copy-start.5 = (bf16[640,1024]{1,0:T(8,128)(2,1)S(1)}, bf16[640,1024]{1,0:T(8,128)(2,1)}, u32[]{:S(2)}) copy-start(bf16[640,1024]{1,0:T(8,128)(2,1)} %all-gather.9.cloned.1.call-done) | copy-start | bytes 3932164
  185.9 68.0 %reduce-scatter.5.cloned.1.call-start = ((), (), s32[]{:S(2)}) async-start(), calls=%async_computation.8 | async-start | bytes 2949120 | tf_op jit(solution)/shard_map/reduce_scatter | solution.py:62
  191.2 22.6 %copy-start = (bf16[160,1024]{1,0:T(8,128)(2,1)S(1)}, bf16[160,1024]{1,0:T(8,128)(2,1)}, u32[]{:S(2)}) copy-start(bf16[160,1024]{1,0:T(8,128)(2,1)} %param.6) | copy-start | bytes 983044
  191.2 62.8 %copy-start.1 = (bf16[160,1024]{1,0:T(8,128)(2,1)S(1)}, bf16[160,1024]{1,0:T(8,128)(2,1)}, u32[]{:S(2)}) copy-start(bf16[160,1024]{1,0:T(8,128)(2,1)} %param.7) | copy-start | bytes 983044
Sparse Core Ops, SparseCore 0:
  9.8 33.6 all-gather.4
  45.9 28.6 all-gather.8
  76.3 33.6 all-gather.10
  112.1 32.8 all-gather.6
  186.0 27.6 reduce-scatter.2
  215.9 37.9 reduce-scatter.4
where the time goes:
time: 266 us; the launch traced here: 265 us
  waiting for transfers between devices  153 us (58%)
  blocking collectives  52.9 us (20%)
  other arithmetic  22 us (8%)
  matrix products  18.1 us (7%)
  between operations  17.3 us (7%)
    reduce_scatter x1, waiting for transfers between devices, on_device(): lax.psum_scatter(jnp.einsum('rc,re->ce', grad_logits, simg, preferred_ele...  37 us
    all_gather x1, waiting for transfers between devices, on_device(): lax.all_gather(stxt_own, 'row', axis=0, tiled=True)  35.4 us
    all_gather x1, waiting for transfers between devices, on_device(): lax.all_gather(ttxt_own, 'row', axis=0, tiled=True)  30.8 us
    all_gather x1, waiting for transfers between devices, on_device(): simg = lax.all_gather(simg_own, 'loop', axis=0, tiled=True)  29.5 us
    all_to_all x1, blocking collectives, on_device(): lax.all_to_all(teacher_text, 'loop', split_axis=0, concat_axis=1, tiled=T...  14.7 us
    psum x1, blocking collectives, on_device(): group_total = lax.psum(jnp.sum(diverge), 'row')  14.2 us
    psum x1, blocking collectives, on_device(): lax.psum((jnp.sum(sexp, axis=1), jnp.sum(texp, axis=1), jnp.sum(texp * (t...  14 us
    all_gather x1, waiting for transfers between devices, on_device(): timg_full = lax.all_gather(teacher_image, 'loop', axis=1, tiled=True)  12.3 us
  transfers between devices with their start and end apart: 6, of which 6 were waited for; matrix products, arithmetic and copies ran while one was open for 8% of the time, Pallas kernels for 0%

commit v1 on v0

v1 whole, which is shorter than its diff:
```python
import functools
import jax
import jax.numpy as jnp
from jax import lax
from jax.experimental import pallas as pl
from jax.experimental.pallas import tpu as pltpu
from jax.sharding import PartitionSpec as P

EPS = 1e-06
F32 = jnp.float32
BF16 = jnp.bfloat16
MESH = pl.DeviceIdType.MESH
STEP = 32


class Ids:
    def __init__(self):
        self.table = {}
        self.count = 0

    def take(self, name, size=1):
        self.table[name] = self.count
        self.count += size

    def __getitem__(self, name):
        return self.table[name]


def make_ids(n_loop, n_kh, n_kl, n_lx, n_ly):
    ids = Ids()
    ids.take("t_img", n_loop)
    ids.take("t_txt", n_loop)
    for a in range(2):
        ids.take(("iz", a), n_kl)
        ids.take(("iy", a), n_ly * n_kl)
        ids.take(("tz", a), n_kh)
        ids.take(("tx", a), n_lx * n_kh)
        ids.take(("tc", a), n_lx * n_kh)
    ids.take("stat", n_kl * n_ly)
    ids.take("dc", n_lx * n_kh)
    ids.take("dx", n_lx * n_kh)
    ids.take("dz", n_kh)
    ids.take("gy", n_ly * n_kl)
    ids.take("gz", n_kl)
    ids.take("lk", n_kh)
    ids.take("lx", n_lx)
    ids.take("lc", 1)
    return ids


def kernel(
    dims, ids,
    si, st, ti, tt, ssc, tsc,
    loss_out, gi_out, gt_out,
    img_s, img_t, own_s, own_t, txt_s, txt_t, raw_i, raw_t,
    slog, tlog, grad, stat, dimg_acc, r1, r2, r3, ry, rz, part,
    ss, rs,
):
    n_row, n_loop, n_kh, n_kl, n_lx, n_ly, D, code = dims
    n_img = n_kl * n_ly
    n_txt = n_kh * n_lx * 2
    rows = n_img * D
    cols = n_txt * D
    feat = code // n_loop
    r = lax.axis_index("row")
    l = lax.axis_index("loop")
    k, c = r // 2, r % 2
    kh, kl = k // n_kl, k % n_kl
    src_kl, src_j = k // n_kh, k % n_kh
    ly, lx = l // n_lx, l % n_lx
    sscale = ssc[0]
    tscale = tsc[0]

    def dev(k_=None, c_=None, ly_=None, lx_=None):
        kk = k if k_ is None else k_
        cc = c if c_ is None else c_
        yy = ly if ly_ is None else ly_
        xx = lx if lx_ is None else lx_
        return (kk * 2 + cc, yy * n_lx + xx)

    def piece(ref, slot):
        return ref.at[pl.ds(pl.multiple_of(slot * D, D), D), :]

    def at(slot):
        return pl.ds(pl.multiple_of(slot * D, D), D)

    def copy(src, dst, q_send, q_recv, device):
        return pltpu.make_async_remote_copy(
            src_ref=src, dst_ref=dst, send_sem=ss.at[q_send], recv_sem=rs.at[q_recv],
            device_id=device, device_id_type=MESH,
        )

    sent = []

    def send(src, dst, q_send, q_recv, device):
        op = copy(src, dst, q_send, q_recv, device)
        op.start()
        sent.append(op)

    def got(dst, q):
        copy(dst, dst, q, q, dev(c_=1 - c)).wait_recv()

    def drain():
        for op in sent:
            op.wait_send()
        sent.clear()

    barrier = pltpu.get_barrier_semaphore()
    n_peer = 0
    for d in range(1, n_loop):
        pl.semaphore_signal(barrier, inc=1, device_id=(r, (l + d) % n_loop), device_id_type=MESH)
        n_peer += 1
    for d in range(1, n_kh * n_kl):
        pl.semaphore_signal(barrier, inc=1, device_id=dev(k_=(k + d) % (n_kh * n_kl)), device_id_type=MESH)
        n_peer += 1
    pl.semaphore_signal(barrier, inc=1, device_id=dev(c_=1 - c), device_id_type=MESH)
    n_peer += 1
    for d in range(1, n_kl):
        for e in range(1, n_ly):
            diagonal = dev(k_=kh * n_kl + (kl + d) % n_kl, ly_=(ly + e) % n_ly)
            pl.semaphore_signal(barrier, inc=1, device_id=diagonal, device_id_type=MESH)
            n_peer += 1
    pl.semaphore_wait(barrier, n_peer)

    slot0 = kl * n_ly + ly

    def islot(kl_, ly_):
        return kl_ * n_ly + ly_

    def tslot(j, lx_, c_):
        return (j * n_lx + lx_) * 2 + c_

    def inv_norm(x):
        n2 = jnp.sum(x * x, axis=1, keepdims=True) + EPS
        n = jnp.sqrt(n2)
        return n, 1.0 / n

    HALF = 32

    def unit_to(src, dst, base):
        def body(i, _):
            o = pl.multiple_of(i * HALF, HALF)
            x = src[pl.ds(o, HALF), :].astype(F32)
            _, inv = inv_norm(x)
            dst[pl.ds(pl.multiple_of(base + o, HALF), HALF), :] = (x * inv).astype(BF16)
            return 0
        lax.fori_loop(0, D // HALF, body, 0)

    def a2a(src, raw, base):
        for d in range(1, n_loop):
            peer = (l + d) % n_loop
            send(piece(src, peer), raw.at[l], base + d, base + d, (r, peer))

    def image_first(a, buf):
        for d in range(1, n_kl):
            p = (kl + d) % n_kl
            q = ids[("iz", a)] + d
            send(piece(buf, slot0), piece(buf, slot0), q, q, dev(k_=kh * n_kl + p))
        for e in range(1, n_ly):
            q = ids[("iy", a)] + e * n_kl
            send(piece(buf, slot0), piece(buf, slot0), q, q, dev(ly_=(ly + e) % n_ly))

    def image_relay(a, buf):
        for d in range(1, n_kl):
            s = islot((kl + n_kl - d) % n_kl, ly)
            got(piece(buf, s), ids[("iz", a)] + d)
            for e in range(1, n_ly):
                q = ids[("iy", a)] + e * n_kl + d
                send(piece(buf, s), piece(buf, s), q, q, dev(ly_=(ly + e) % n_ly))

    def image_finish(a, buf):
        for e in range(1, n_ly):
            for d in range(n_kl):
                s = islot((kl + n_kl - d) % n_kl, (ly + n_ly - e) % n_ly)
                got(piece(buf, s), ids[("iy", a)] + e * n_kl + d)

    def text_first(a, own, buf):
        s = tslot(src_j, lx, c)
        for h in range(n_kh):
            dest = h * n_kl + src_kl
            op = copy(own, piece(buf, s), ids[("tz", a)] + h, ids[("tz", a)] + src_j, dev(k_=dest))

            @pl.when(dest != k)
            def _():
                op.start()

            @pl.when(dest == k)
            def _():
                buf[at(s), :] = own[...]

    def text_first_drain(a, own, buf):
        s = tslot(src_j, lx, c)
        for h in range(n_kh):
            dest = h * n_kl + src_kl
            op = copy(own, piece(buf, s), ids[("tz", a)] + h, ids[("tz", a)] + src_j, dev(k_=dest))

            @pl.when(dest != k)
            def _():
                op.wait_send()

    def text_relay(a, buf):
        for j in range(n_kh):
            s = tslot(j, lx, c)

            @pl.when(kl * n_kh + j != k)
            def _():
                got(piece(buf, s), ids[("tz", a)] + j)

            for e in range(1, n_lx):
                q = ids[("tx", a)] + e * n_kh + j
                send(piece(buf, s), piece(buf, s), q, q, dev(lx_=(lx + e) % n_lx))
            q = ids[("tc", a)] + j
            send(piece(buf, s), piece(buf, s), q, q, dev(c_=1 - c))

    def text_cross(a, buf):
        for e in range(1, n_lx):
            for j in range(n_kh):
                s = tslot(j, (lx + n_lx - e) % n_lx, c)
                got(piece(buf, s), ids[("tx", a)] + e * n_kh + j)
                q = ids[("tc", a)] + e * n_kh + j
                send(piece(buf, s), piece(buf, s), q, q, dev(c_=1 - c))

    def text_finish(a, buf):
        for e in range(n_lx):
            for j in range(n_kh):
                s = tslot(j, (lx + n_lx - e) % n_lx, 1 - c)
                got(piece(buf, s), ids[("tc", a)] + e * n_kh + j)

    def teacher_unit(src, raw, base_id, dst, base):
        raw[l] = src[at(l), :]
        for d in range(1, n_loop):
            got(raw.at[(l + n_loop - d) % n_loop], base_id + d)

        def body(i, _):
            o = pl.multiple_of(i * HALF, HALF)
            xs = [raw[f, pl.ds(o, HALF), :].astype(F32) for f in range(n_loop)]
            x = jnp.concatenate(xs, axis=1)
            _, inv = inv_norm(x)
            dst[pl.ds(pl.multiple_of(base + o, HALF), HALF), :] = (x * inv).astype(BF16)
            return 0
        lax.fori_loop(0, D // HALF, body, 0)

    a2a(ti, raw_i, ids["t_img"])
    a2a(tt, raw_t, ids["t_txt"])
    unit_to(st, own_s, 0)
    text_first(0, own_s, txt_s)
    unit_to(si, img_s, slot0 * D)
    image_first(0, img_s)
    teacher_unit(tt, raw_t, ids["t_txt"], own_t, 0)
    text_first(1, own_t, txt_t)
    teacher_unit(ti, raw_i, ids["t_img"], img_t, slot0 * D)
    image_first(1, img_t)
    image_relay(0, img_s)
    text_relay(0, txt_s)
    text_cross(0, txt_s)
    image_relay(1, img_t)
    text_relay(1, txt_t)
    image_finish(0, img_s)
    text_finish(0, txt_s)

    TILE = 2 * D

    def logits(txt, img, scale, out):
        def body(i, m):
            o = pl.multiple_of(i * TILE, TILE)
            v = scale * lax.dot_general(
                txt[pl.ds(o, TILE), :], img[...], (((1,), (1,)), ((), ())),
                preferred_element_type=F32,
            )
            out[pl.ds(o, TILE), :] = v
            return jnp.maximum(m, jnp.max(v.reshape(TILE // 8, 8, rows), axis=0))
        m = lax.fori_loop(0, cols // TILE, body, jnp.full((8, rows), -jnp.inf, F32))
        return jnp.max(m, axis=0, keepdims=True)

    smax = logits(txt_s, img_s, sscale, slog)
    text_cross(1, txt_t)
    image_finish(1, img_t)
    text_finish(1, txt_t)
    tmax = logits(txt_t, img_t, tscale, tlog)

    def exps(i, carry):
        a, b, x = carry
        o = pl.multiple_of(i * STEP, STEP)
        s = slog[pl.ds(o, STEP), :]
        t = tlog[pl.ds(o, STEP), :]
        es = jnp.exp(s - smax)
        et = jnp.exp(t - tmax)
        slog[pl.ds(o, STEP), :] = es
        tlog[pl.ds(o, STEP), :] = et

        def fold(v):
            return jnp.sum(v.reshape(STEP // 8, 8, rows), axis=0)
        return (a + fold(es), b + fold(et), x + fold(et * (t - s)))

    zero = jnp.zeros((8, rows), F32)
    asum, bsum, xsum = lax.fori_loop(0, cols // STEP, exps, (zero, zero, zero))
    pack = [smax, tmax] + [jnp.sum(v, axis=0, keepdims=True) for v in (asum, bsum, xsum)]
    stat[slot0] = jnp.concatenate(pack + [jnp.zeros((3, rows), F32)], axis=0)
    for d in range(n_kl):
        for e in range(n_ly):
            if d or e:
                q = ids["stat"] + d * n_ly + e
                send(stat.at[slot0], stat.at[slot0], q, q,
                     dev(k_=kh * n_kl + (kl + d) % n_kl, ly_=(ly + e) % n_ly))
    for d in range(n_kl):
        for e in range(n_ly):
            if d or e:
                s = islot((kl + n_kl - d) % n_kl, (ly + n_ly - e) % n_ly)
                got(stat.at[s], ids["stat"] + d * n_ly + e)

    all_stat = [stat[s] for s in range(n_img)]
    gs = functools.reduce(jnp.maximum, [v[0:1] for v in all_stat])
    gt = functools.reduce(jnp.maximum, [v[1:2] for v in all_stat])
    es = [jnp.exp(v[0:1] - gs) for v in all_stat]
    et = [jnp.exp(v[1:2] - gt) for v in all_stat]
    ssum = sum(v[2:3] * e for v, e in zip(all_stat, es))
    tsum = sum(v[3:4] * e for v, e in zip(all_stat, et))
    cross = sum(v[4:5] * e for v, e in zip(all_stat, et))
    diverge = cross / tsum - (gt + jnp.log(tsum)) + (gs + jnp.log(ssum))
    s_mul = sscale * jnp.exp(smax - gs) / ssum
    t_mul = sscale * jnp.exp(tmax - gt) / tsum

    def to_grad(i, _):
        o = pl.multiple_of(i * STEP, STEP)
        v = slog[pl.ds(o, STEP), :] * s_mul - tlog[pl.ds(o, STEP), :] * t_mul
        grad[pl.ds(o, STEP), :] = v.astype(BF16)
        return 0
    lax.fori_loop(0, cols // STEP, to_grad, 0)

    drain()
    for a, own, buf in ((0, own_s, txt_s), (1, own_t, txt_t)):
        text_first_drain(a, own, buf)
    dtxt = txt_t

    def dtxt_pieces(lx_, c_):
        def body(j, _):
            rng = at(tslot(j, lx_, c_))
            dtxt[rng, :] = jnp.dot(grad[rng, :], img_s[...], preferred_element_type=F32).astype(BF16)
            return 0
        lax.fori_loop(0, n_kh, body, 0)

    for e in [*range(1, n_lx), 0]:
        x_ = (lx + e) % n_lx
        dtxt_pieces(x_, 1 - c)
        for j in range(n_kh):
            q = ids["dc"] + e * n_kh + j
            send(piece(dtxt, tslot(j, x_, 1 - c)), r1.at[x_ * n_kh + j], q, q, dev(c_=1 - c))
    for e in range(1, n_lx):
        x_ = (lx + e) % n_lx
        dtxt_pieces(x_, c)
        for j in range(n_kh):
            got(r1.at[x_ * n_kh + j], ids["dc"] + e * n_kh + j)
            rng = at(tslot(j, x_, c))
            dtxt[rng, :] = (dtxt[rng, :].astype(F32) + r1[x_ * n_kh + j].astype(F32)).astype(BF16)
            q = ids["dx"] + e * n_kh + j
            send(piece(dtxt, tslot(j, x_, c)), r2.at[(e - 1) * n_kh + j], q, q, dev(lx_=x_))

    KT = 256
    dimg_acc[...] = jnp.zeros_like(dimg_acc)

    def dimg_body(i, _):
        o = pl.multiple_of(i * KT, KT)
        dimg_acc[...] += lax.dot_general(
            grad[pl.ds(o, KT), :], txt_s[pl.ds(o, KT), :], (((0,), (0,)), ((), ())),
            preferred_element_type=F32,
        )
        return 0
    lax.fori_loop(0, cols // KT, dimg_body, 0)
    dimg = img_t
    for s in range(n_img):
        dimg[pl.ds(s * D, D), :] = dimg_acc[pl.ds(s * D, D), :].astype(BF16)
    for e in range(1, n_ly):
        y_ = (ly + e) % n_ly
        for d in range(n_kl):
            q = ids["gy"] + e * n_kl + d
            send(piece(dimg, islot((kl + d) % n_kl, y_)), ry.at[(e - 1) * n_kl + d], q, q, dev(ly_=y_))

    dtxt_pieces(lx, c)

    for j in range(n_kh):
        got(r1.at[lx * n_kh + j], ids["dc"] + j)
        v = dtxt[at(tslot(j, lx, c)), :].astype(F32) + r1[lx * n_kh + j].astype(F32)
        for e in range(1, n_lx):
            got(r2.at[(e - 1) * n_kh + j], ids["dx"] + e * n_kh + j)
            v = v + r2[(e - 1) * n_kh + j].astype(F32)
        z_rng = at(tslot(j, lx, c))
        dtxt[z_rng, :] = v.astype(BF16)
        dest = kl * n_kh + j
        op = copy(piece(dtxt, tslot(j, lx, c)), r3.at[kh], ids["dz"] + j, ids["dz"] + kh, dev(k_=dest))

        @pl.when(dest != k)
        def _():
            op.start()

        @pl.when(dest == k)
        def _():
            r3[kh] = dtxt[z_rng, :]

    def image_sum(d):
        v = dimg[at(islot((kl + d) % n_kl, ly)), :].astype(F32)
        for e in range(1, n_ly):
            v = v + ry[(e - 1) * n_kl + d].astype(F32)
        return v

    for e in range(1, n_ly):
        for d in range(n_kl):
            got(ry.at[(e - 1) * n_kl + d], ids["gy"] + e * n_kl + d)
    for d in range(1, n_kl):
        pair_slot = islot((kl + d) % n_kl, ly)
        dimg[at(pair_slot), :] = image_sum(d).astype(BF16)
        q = ids["gz"] + d
        send(piece(dimg, pair_slot), rz.at[d - 1], q, q, dev(k_=kh * n_kl + (kl + d) % n_kl))

    total = jnp.broadcast_to(jnp.sum(diverge, axis=1, keepdims=True), (8, 128))
    part[kh] = total
    for d in range(1, n_kh):
        q = ids["lk"] + d
        send(part.at[kh], part.at[kh], q, q, dev(k_=((kh + d) % n_kh) * n_kl + kl))
    for d in range(1, n_kh):
        got(part.at[(kh + n_kh - d) % n_kh], ids["lk"] + d)
    base = n_kh
    total = sum(part[i] for i in range(n_kh))
    part[base + lx] = total
    for d in range(1, n_lx):
        q = ids["lx"] + d
        send(part.at[base + lx], part.at[base + lx], q, q, dev(lx_=(lx + d) % n_lx))
    for d in range(1, n_lx):
        got(part.at[base + (lx + n_lx - d) % n_lx], ids["lx"] + d)
    total = sum(part[base + i] for i in range(n_lx))
    base = n_kh + n_lx
    part[base + c] = total
    send(part.at[base + c], part.at[base + c], ids["lc"], ids["lc"], dev(c_=1 - c))
    got(part.at[base + 1 - c], ids["lc"])
    total = part[base] + part[base + 1]
    loss_out[...] = total / float(D * n_row * n_loop)

    def finish(src, terms, out):
        def body(i, _):
            rng = pl.ds(pl.multiple_of(i * HALF, HALF), HALF)
            x = src[rng, :].astype(F32)
            n, inv = inv_norm(x)
            u = x * inv
            g = terms(rng)
            inner = jnp.sum(g * u, axis=1, keepdims=True)
            out[rng, :] = ((g - u * inner) * inv).astype(BF16)
            return 0
        lax.fori_loop(0, D // HALF, body, 0)

    for d in range(1, n_kl):
        got(rz.at[d - 1], ids["gz"] + d)

    def image_terms(rng):
        o = pl.multiple_of(slot0 * D + rng.start, HALF)
        v = dimg[pl.ds(o, HALF), :].astype(F32)
        for e in range(1, n_ly):
            v = v + ry[(e - 1) * n_kl, rng, :].astype(F32)
        for d in range(1, n_kl):
            v = v + rz[d - 1, rng, :].astype(F32)
        return v
    finish(si, image_terms, gi_out)

    for h in range(n_kh):
        @pl.when(h * n_kl + src_kl != k)
        def _():
            got(r3.at[h], ids["dz"] + h)
    finish(st, lambda rng: sum(r3[h, rng, :].astype(F32) for h in range(n_kh)), gt_out)

    drain()
    for j in range(n_kh):
        dest = kl * n_kh + j
        op = copy(piece(dtxt, tslot(j, lx, c)), r3.at[kh], ids["dz"] + j, ids["dz"] + kh, dev(k_=dest))

        @pl.when(dest != k)
        def _():
            op.wait_send()


def on_device(n_row, n_loop, si, st, ti, tt, ssc, tsc):
    D, code = si.shape
    n_kl, n_lx = 2, 2
    n_kh, n_ly = n_row // (2 * n_kl), n_loop // n_lx
    n_img, n_txt = n_kl * n_ly, n_kh * n_lx * 2
    rows, cols = n_img * D, n_txt * D
    ids = make_ids(n_loop, n_kh, n_kl, n_lx, n_ly)
    dims = (n_row, n_loop, n_kh, n_kl, n_lx, n_ly, D, code)
    vm = pl.BlockSpec(memory_space=pltpu.VMEM)
    sm = pl.BlockSpec(memory_space=pltpu.SMEM)
    V = pltpu.VMEM
    loss, gi, gt = pl.pallas_call(
        functools.partial(kernel, dims, ids),
        out_shape=(
            jax.ShapeDtypeStruct((8, 128), F32),
            jax.ShapeDtypeStruct((D, code), BF16),
            jax.ShapeDtypeStruct((D, code), BF16),
        ),
        in_specs=[vm] * 4 + [sm] * 2,
        out_specs=(vm, vm, vm),
        scratch_shapes=[
            V((rows, code), BF16), V((rows, code), BF16),
            V((D, code), BF16), V((D, code), BF16),
            V((cols, code), BF16), V((cols, code), BF16),
            V((n_loop, D, code // n_loop), BF16), V((n_loop, D, code // n_loop), BF16),
            V((cols, rows), F32), V((cols, rows), F32), V((cols, rows), BF16),
            V((n_img, 8, rows), F32),
            V((rows, code), F32),
            V((n_lx * n_kh, D, code), BF16),
            V(((n_lx - 1) * n_kh, D, code), BF16),
            V((n_kh, D, code), BF16),
            V(((n_ly - 1) * n_kl, D, code), BF16),
            V((n_kl - 1, D, code), BF16),
            V((n_kh + n_lx + 2, 8, 128), F32),
            pltpu.SemaphoreType.DMA((ids.count,)),
            pltpu.SemaphoreType.DMA((ids.count,)),
        ],
        compiler_params=pltpu.CompilerParams(
            collective_id=0, has_side_effects=True, vmem_limit_bytes=67043328,
        ),
    )(si, st, ti, tt, ssc, tsc)
    return loss[0, :1], gi, gt


def solution(mesh):
    return jax.shard_map(
        functools.partial(on_device, mesh.shape["row"], mesh.shape["loop"]),
        mesh=mesh,
        in_specs=(
            P(("row", "loop"), None),
            P(("row", "loop"), None),
            P("row", "loop"),
            P("row", "loop"),
            P(),
            P(),
        ),
        out_specs=(P(), P(("row", "loop"), None), P(("row", "loop"), None)),
        check_vma=False,
    )
```

time: 266 us -> 110 us (0.41)
  the two profiles are of different devices: /device:TPU:0 before, /device:TPU:21 now
where the time goes in v1:
time: 110 us; the launch traced here: 109 us
  Pallas kernels  103 us (94%)
  local copies, waits for them, and re-layouts  3.67 us (3%)
  between operations  1.93 us (2%)
    pallas_call x1, Pallas kernels, on_device(): pl.pallas_call(functools.partial(kernel, dims, ids), out_shape=(jax.Shape...  103 us
    unnamed x4, local copies, waits for them, and re-layouts  2.49 us

profile of v1, /device:TPU:21, one launch (start us, length us, event | category | flops | bytes accessed | tf_op | source)
XLA Modules:
  0.0 108.7 jit_solution(6775180935991941863)
XLA Ops:
  1.9 103.1 %shard_map.85 = (f32[8,128]{1,0:T(8,128)}, bf16[160,1024]{1,0:T(8,128)(2,1)}, bf16[160,1024]{1,0:T(8,128)(2,1)}) custom-call(bf16[160,1024]{1,0:T(8,128)(2,1)} %si.1, bf16[160,1024]{1,0:T(8,128)(2,1)} %st.1, bf16[640,256]{1,0:T(8,128)(2,1)} %ti.1, bf16[640,256]{1,0:T(8,128)(2,1)} %tt.1, f32[1]{0:T(128)S(6)} %copy.11.ssc, f32[1]{0:T(128)S(6)} %copy.12.tsc), custom_call_target="tpu_custom_call" | custom-call | tf_op jit(solution)/shard_map/pallas_call | solution.py:489
  105.0 1.2 %slice.3 = f32[1,1]{1,0:T(1,128)} slice(f32[8,128]{1,0:T(8,128)} %get-tuple-element.6), slice={[0:1], [0:1]} | slice | bytes 8 | tf_op jit(solution)/shard_map/slice | solution.py:519
  106.2 0.0 copy-start
  106.2 1.8 %copy.13 = bf16[160,1024]{1,0:T(8,128)(2,1)} copy(bf16[160,1024]{1,0:T(8,128)(2,1)} %get-tuple-element.13) | data formatting | bytes 655360
  107.9 0.0 copy-done
  107.9 0.7 copy.14
Async XLA Ops:
  106.2 1.8 %copy-start = (bf16[160,1024]{1,0:T(8,128)(2,1)S(1)}, bf16[160,1024]{1,0:T(8,128)(2,1)}, u32[]{:S(2)}) copy-start(bf16[160,1024]{1,0:T(8,128)(2,1)} %get-tuple-element.14) | copy-start | bytes 983044

commit v2 on v1

--- a/solution.py
+++ b/solution.py
@@ -11,6 +11,7 @@
 BF16 = jnp.bfloat16
 MESH = pl.DeviceIdType.MESH
 STEP = 32
+CHUNKS = 2
 
 
 class Ids:
@@ -31,17 +32,17 @@
     ids.take("t_img", n_loop)
     ids.take("t_txt", n_loop)
     for a in range(2):
-        ids.take(("iz", a), n_kl)
-        ids.take(("iy", a), n_ly * n_kl)
-        ids.take(("tz", a), n_kh)
-        ids.take(("tx", a), n_lx * n_kh)
-        ids.take(("tc", a), n_lx * n_kh)
+        ids.take(("iz", a), n_kl * CHUNKS)
+        ids.take(("iy", a), n_ly * n_kl * CHUNKS)
+        ids.take(("tz", a), n_kh * CHUNKS)
+        ids.take(("tx", a), n_lx * n_kh * CHUNKS)
+        ids.take(("tc", a), n_lx * n_kh * CHUNKS)
     ids.take("stat", n_kl * n_ly)
-    ids.take("dc", n_lx * n_kh)
-    ids.take("dx", n_lx * n_kh)
-    ids.take("dz", n_kh)
-    ids.take("gy", n_ly * n_kl)
-    ids.take("gz", n_kl)
+    ids.take("dc", n_lx * n_kh * CHUNKS)
+    ids.take("dx", n_lx * n_kh * CHUNKS)
+    ids.take("dz", n_kh * CHUNKS)
+    ids.take("gy", n_ly * n_kl * CHUNKS)
+    ids.take("gz", n_kl * CHUNKS)
     ids.take("lk", n_kh)
     ids.take("lx", n_lx)
     ids.take("lc", 1)
@@ -60,6 +61,7 @@
     n_img = n_kl * n_ly
     n_txt = n_kh * n_lx * 2
     rows = n_img * D
+    Dc = D // CHUNKS
     cols = n_txt * D
     feat = code // n_loop
     r = lax.axis_index("row")
@@ -80,6 +82,12 @@
 
     def piece(ref, slot):
         return ref.at[pl.ds(pl.multiple_of(slot * D, D), D), :]
+
+    def chunk(ref, slot, h):
+        return ref.at[pl.ds(pl.multiple_of(slot * D + h * Dc, Dc), Dc), :]
+
+    def chunk_of(ref, i, h):
+        return ref.at[i, pl.ds(h * Dc, Dc), :]
 
     def at(slot):
         return pl.ds(pl.multiple_of(slot * D, D), D)
@@ -135,50 +143,57 @@
         n = jnp.sqrt(n2)
         return n, 1.0 / n
 
-    HALF = 32
-
-    def unit_to(src, dst, base):
+    HALF = 16
+
+    def unit_to(src, dst, base, h):
         def body(i, _):
-            o = pl.multiple_of(i * HALF, HALF)
+            o = pl.multiple_of(h * Dc + i * HALF, HALF)
             x = src[pl.ds(o, HALF), :].astype(F32)
             _, inv = inv_norm(x)
             dst[pl.ds(pl.multiple_of(base + o, HALF), HALF), :] = (x * inv).astype(BF16)
             return 0
-        lax.fori_loop(0, D // HALF, body, 0)
+        lax.fori_loop(0, Dc // HALF, body, 0)
 
     def a2a(src, raw, base):
         for d in range(1, n_loop):
             peer = (l + d) % n_loop
             send(piece(src, peer), raw.at[l], base + d, base + d, (r, peer))
 
-    def image_first(a, buf):
+    def image_first(a, buf, h):
         for d in range(1, n_kl):
             p = (kl + d) % n_kl
-            q = ids[("iz", a)] + d
-            send(piece(buf, slot0), piece(buf, slot0), q, q, dev(k_=kh * n_kl + p))
+            q = ids[("iz", a)] + d * CHUNKS + h
+            send(chunk(buf, slot0, h), chunk(buf, slot0, h), q, q, dev(k_=kh * n_kl + p))
         for e in range(1, n_ly):
-            q = ids[("iy", a)] + e * n_kl
-            send(piece(buf, slot0), piece(buf, slot0), q, q, dev(ly_=(ly + e) % n_ly))
-
-    def image_relay(a, buf):
+            q = ids[("iy", a)] + e * n_kl * CHUNKS + h
+            send(chunk(buf, slot0, h), chunk(buf, slot0, h), q, q, dev(ly_=(ly + e) % n_ly))
+
+    def image_relay(a, buf, h):
         for d in range(1, n_kl):
             s = islot((kl + n_kl - d) % n_kl, ly)
-            got(piece(buf, s), ids[("iz", a)] + d)
+            got(chunk(buf, s, h), ids[("iz", a)] + d * CHUNKS + h)
             for e in range(1, n_ly):
-                q = ids[("iy", a)] + e * n_kl + d
-                send(piece(buf, s), piece(buf, s), q, q, dev(ly_=(ly + e) % n_ly))
+                q = ids[("iy", a)] + (e * n_kl + d) * CHUNKS + h
+                send(chunk(buf, s, h), chunk(buf, s, h), q, q, dev(ly_=(ly + e) % n_ly))
 
     def image_finish(a, buf):
-        for e in range(1, n_ly):
-            for d in range(n_kl):
-                s = islot((kl + n_kl - d) % n_kl, (ly + n_ly - e) % n_ly)
-                got(piece(buf, s), ids[("iy", a)] + e * n_kl + d)
-
-    def text_first(a, own, buf):
+        for h in range(CHUNKS):
+            for e in range(1, n_ly):
+                for d in range(n_kl):
+                    s = islot((kl + n_kl - d) % n_kl, (ly + n_ly - e) % n_ly)
+                    got(chunk(buf, s, h), ids[("iy", a)] + (e * n_kl + d) * CHUNKS + h)
+
+    def text_first_copy(a, own, buf, h, g):
+        dest = g * n_kl + src_kl
+        q = ids[("tz", a)]
         s = tslot(src_j, lx, c)
-        for h in range(n_kh):
-            dest = h * n_kl + src_kl
-            op = copy(own, piece(buf, s), ids[("tz", a)] + h, ids[("tz", a)] + src_j, dev(k_=dest))
+        op = copy(chunk(own, 0, h), chunk(buf, s, h), q + g * CHUNKS + h,
+                  q + src_j * CHUNKS + h, dev(k_=dest))
+        return dest, op
+
+    def text_first(a, own, buf, h):
+        for g in range(n_kh):
+            dest, op = text_first_copy(a, own, buf, h, g)
 
             @pl.when(dest != k)
             def _():
@@ -186,75 +201,84 @@
 
             @pl.when(dest == k)
             def _():
-                buf[at(s), :] = own[...]
+                o = pl.multiple_of(tslot(src_j, lx, c) * D + h * Dc, Dc)
+                buf[pl.ds(o, Dc), :] = own[pl.ds(h * Dc, Dc), :]
 
     def text_first_drain(a, own, buf):
-        s = tslot(src_j, lx, c)
-        for h in range(n_kh):
-            dest = h * n_kl + src_kl
-            op = copy(own, piece(buf, s), ids[("tz", a)] + h, ids[("tz", a)] + src_j, dev(k_=dest))
-
-            @pl.when(dest != k)
-            def _():
-                op.wait_send()
-
-    def text_relay(a, buf):
+        for h in range(CHUNKS):
+            for g in range(n_kh):
+                dest, op = text_first_copy(a, own, buf, h, g)
+
+                @pl.when(dest != k)
+                def _():
+                    op.wait_send()
+
+    def text_relay(a, buf, h):
         for j in range(n_kh):
             s = tslot(j, lx, c)
 
             @pl.when(kl * n_kh + j != k)
             def _():
-                got(piece(buf, s), ids[("tz", a)] + j)
+                got(chunk(buf, s, h), ids[("tz", a)] + j * CHUNKS + h)
 
             for e in range(1, n_lx):
-                q = ids[("tx", a)] + e * n_kh + j
-                send(piece(buf, s), piece(buf, s), q, q, dev(lx_=(lx + e) % n_lx))
-            q = ids[("tc", a)] + j
-            send(piece(buf, s), piece(buf, s), q, q, dev(c_=1 - c))
-
-    def text_cross(a, buf):
+                q = ids[("tx", a)] + (e * n_kh + j) * CHUNKS + h
+                send(chunk(buf, s, h), chunk(buf, s, h), q, q, dev(lx_=(lx + e) % n_lx))
+            q = ids[("tc", a)] + j * CHUNKS + h
+            send(chunk(buf, s, h), chunk(buf, s, h), q, q, dev(c_=1 - c))
+
+    def text_cross(a, buf, h):
         for e in range(1, n_lx):
             for j in range(n_kh):
                 s = tslot(j, (lx + n_lx - e) % n_lx, c)
-                got(piece(buf, s), ids[("tx", a)] + e * n_kh + j)
-                q = ids[("tc", a)] + e * n_kh + j
-                send(piece(buf, s), piece(buf, s), q, q, dev(c_=1 - c))
+                got(chunk(buf, s, h), ids[("tx", a)] + (e * n_kh + j) * CHUNKS + h)
+                q = ids[("tc", a)] + (e * n_kh + j) * CHUNKS + h
+                send(chunk(buf, s, h), chunk(buf, s, h), q, q, dev(c_=1 - c))
 
     def text_finish(a, buf):
-        for e in range(n_lx):
-            for j in range(n_kh):
-                s = tslot(j, (lx + n_lx - e) % n_lx, 1 - c)
-                got(piece(buf, s), ids[("tc", a)] + e * n_kh + j)
-
-    def teacher_unit(src, raw, base_id, dst, base):
+        for h in range(CHUNKS):
+            for e in range(n_lx):
+                for j in range(n_kh):
+                    s = tslot(j, (lx + n_lx - e) % n_lx, 1 - c)
+                    got(chunk(buf, s, h), ids[("tc", a)] + (e * n_kh + j) * CHUNKS + h)
+
+    def teacher_wait(src, raw, base_id):
         raw[l] = src[at(l), :]
         for d in range(1, n_loop):
             got(raw.at[(l + n_loop - d) % n_loop], base_id + d)
 
+    def teacher_unit(raw, dst, base, h):
         def body(i, _):
-            o = pl.multiple_of(i * HALF, HALF)
+            o = pl.multiple_of(h * Dc + i * HALF, HALF)
             xs = [raw[f, pl.ds(o, HALF), :].astype(F32) for f in range(n_loop)]
             x = jnp.concatenate(xs, axis=1)
             _, inv = inv_norm(x)
             dst[pl.ds(pl.multiple_of(base + o, HALF), HALF), :] = (x * inv).astype(BF16)
             return 0
-        lax.fori_loop(0, D // HALF, body, 0)
-
+        lax.fori_loop(0, Dc // HALF, body, 0)
+
+    a2a(tt, raw_t, ids["t_txt"])
     a2a(ti, raw_i, ids["t_img"])
-    a2a(tt, raw_t, ids["t_txt"])
-    unit_to(st, own_s, 0)
-    text_first(0, own_s, txt_s)
-    unit_to(si, img_s, slot0 * D)
-    image_first(0, img_s)
-    teacher_unit(tt, raw_t, ids["t_txt"], own_t, 0)
-    text_first(1, own_t, txt_t)
-    teacher_unit(ti, raw_i, ids["t_img"], img_t, slot0 * D)
-    image_first(1, img_t)
-    image_relay(0, img_s)
-    text_relay(0, txt_s)
-    text_cross(0, txt_s)
-    image_relay(1, img_t)
-    text_relay(1, txt_t)
+    for h in range(CHUNKS):
+        unit_to(st, own_s, 0, h)
+        text_first(0, own_s, txt_s, h)
+        unit_to(si, img_s, slot0 * D, h)
+        image_first(0, img_s, h)
+    for h in range(CHUNKS):
+        text_relay(0, txt_s, h)
+        image_relay(0, img_s, h)
+        if h == 0:
+            teacher_wait(tt, raw_t, ids["t_txt"])
+        teacher_unit(raw_t, own_t, 0, h)
+        text_first(1, own_t, txt_t, h)
+        if h == 0:
+            teacher_wait(ti, raw_i, ids["t_img"])
+        teacher_unit(raw_i, img_t, slot0 * D, h)
+        image_first(1, img_t, h)
+    for h in range(CHUNKS):
+        text_cross(0, txt_s, h)
+        text_relay(1, txt_t, h)
+        image_relay(1, img_t, h)
     image_finish(0, img_s)
     text_finish(0, txt_s)
 
@@ -273,7 +297,8 @@
         return jnp.max(m, axis=0, keepdims=True)
 
     smax = logits(txt_s, img_s, sscale, slog)
-    text_cross(1, txt_t)
+    for h in range(CHUNKS):
+        text_cross(1, txt_t, h)
     image_finish(1, img_t)
     text_finish(1, txt_t)
     tmax = logits(txt_t, img_t, tscale, tlog)
@@ -339,21 +364,31 @@
             return 0
         lax.fori_loop(0, n_kh, body, 0)
 
-    for e in [*range(1, n_lx), 0]:
+    def to_core(e):
         x_ = (lx + e) % n_lx
         dtxt_pieces(x_, 1 - c)
-        for j in range(n_kh):
-            q = ids["dc"] + e * n_kh + j
-            send(piece(dtxt, tslot(j, x_, 1 - c)), r1.at[x_ * n_kh + j], q, q, dev(c_=1 - c))
+        for h in range(CHUNKS):
+            for j in range(n_kh):
+                q = ids["dc"] + (e * n_kh + j) * CHUNKS + h
+                send(chunk(dtxt, tslot(j, x_, 1 - c), h), chunk_of(r1, x_ * n_kh + j, h), q, q, dev(c_=1 - c))
+
+    def chunk_rows(slot, h):
+        return pl.ds(pl.multiple_of(slot * D + h * Dc, Dc), Dc)
+
+    half = [pl.ds(h * Dc, Dc) for h in range(CHUNKS)]
+
     for e in range(1, n_lx):
         x_ = (lx + e) % n_lx
+        to_core(e)
         dtxt_pieces(x_, c)
-        for j in range(n_kh):
-            got(r1.at[x_ * n_kh + j], ids["dc"] + e * n_kh + j)
-            rng = at(tslot(j, x_, c))
-            dtxt[rng, :] = (dtxt[rng, :].astype(F32) + r1[x_ * n_kh + j].astype(F32)).astype(BF16)
-            q = ids["dx"] + e * n_kh + j
-            send(piece(dtxt, tslot(j, x_, c)), r2.at[(e - 1) * n_kh + j], q, q, dev(lx_=x_))
+        for h in range(CHUNKS):
+            for j in range(n_kh):
+                i = x_ * n_kh + j
+                got(chunk_of(r1, i, h), ids["dc"] + (e * n_kh + j) * CHUNKS + h)
+                rng = chunk_rows(tslot(j, x_, c), h)
+                dtxt[rng, :] = (dtxt[rng, :].astype(F32) + r1[i, half[h], :].astype(F32)).astype(BF16)
+                q = ids["dx"] + (e * n_kh + j) * CHUNKS + h
+                send(chunk(dtxt, tslot(j, x_, c), h), chunk_of(r2, (e - 1) * n_kh + j, h), q, q, dev(lx_=x_))
 
     KT = 256
     dimg_acc[...] = jnp.zeros_like(dimg_acc)
@@ -369,24 +404,31 @@
     dimg = img_t
     for s in range(n_img):
         dimg[pl.ds(s * D, D), :] = dimg_acc[pl.ds(s * D, D), :].astype(BF16)
-    for e in range(1, n_ly):
-        y_ = (ly + e) % n_ly
-        for d in range(n_kl):
-            q = ids["gy"] + e * n_kl + d
-            send(piece(dimg, islot((kl + d) % n_kl, y_)), ry.at[(e - 1) * n_kl + d], q, q, dev(ly_=y_))
-
+    for d in [*range(1, n_kl), 0]:
+        for h in range(CHUNKS):
+            for e in range(1, n_ly):
+                y_ = (ly + e) % n_ly
+                q = ids["gy"] + (e * n_kl + d) * CHUNKS + h
+                send(chunk(dimg, islot((kl + d) % n_kl, y_), h), chunk_of(ry, (e - 1) * n_kl + d, h), q, q, dev(ly_=y_))
+
+    to_core(0)
     dtxt_pieces(lx, c)
 
-    for j in range(n_kh):
-        got(r1.at[lx * n_kh + j], ids["dc"] + j)
-        v = dtxt[at(tslot(j, lx, c)), :].astype(F32) + r1[lx * n_kh + j].astype(F32)
+    def owner_copy(j, h):
+        dest = kl * n_kh + j
+        op = copy(chunk(dtxt, tslot(j, lx, c), h), chunk_of(r3, kh, h),
+                  ids["dz"] + j * CHUNKS + h, ids["dz"] + kh * CHUNKS + h, dev(k_=dest))
+        return dest, op
+
+    def text_sum(j, h):
+        got(chunk_of(r1, lx * n_kh + j, h), ids["dc"] + j * CHUNKS + h)
+        rng = chunk_rows(tslot(j, lx, c), h)
+        v = dtxt[rng, :].astype(F32) + r1[lx * n_kh + j, half[h], :].astype(F32)
         for e in range(1, n_lx):
-            got(r2.at[(e - 1) * n_kh + j], ids["dx"] + e * n_kh + j)
-            v = v + r2[(e - 1) * n_kh + j].astype(F32)
-        z_rng = at(tslot(j, lx, c))
-        dtxt[z_rng, :] = v.astype(BF16)
-        dest = kl * n_kh + j
-        op = copy(piece(dtxt, tslot(j, lx, c)), r3.at[kh], ids["dz"] + j, ids["dz"] + kh, dev(k_=dest))
+            got(chunk_of(r2, (e - 1) * n_kh + j, h), ids["dx"] + (e * n_kh + j) * CHUNKS + h)
+            v = v + r2[(e - 1) * n_kh + j, half[h], :].astype(F32)
+        dtxt[rng, :] = v.astype(BF16)
+        dest, op = owner_copy(j, h)
 
         @pl.when(dest != k)
         def _():
@@ -394,22 +436,30 @@
 
         @pl.when(dest == k)
         def _():
-            r3[kh] = dtxt[z_rng, :]
-
-    def image_sum(d):
-        v = dimg[at(islot((kl + d) % n_kl, ly)), :].astype(F32)
+            r3[kh, half[h], :] = dtxt[rng, :]
+
+    def got_y(d, h):
         for e in range(1, n_ly):
-            v = v + ry[(e - 1) * n_kl + d].astype(F32)
-        return v
-
-    for e in range(1, n_ly):
-        for d in range(n_kl):
-            got(ry.at[(e - 1) * n_kl + d], ids["gy"] + e * n_kl + d)
-    for d in range(1, n_kl):
+            got(chunk_of(ry, (e - 1) * n_kl + d, h), ids["gy"] + (e * n_kl + d) * CHUNKS + h)
+
+    def image_sum(d, h):
+        got_y(d, h)
         pair_slot = islot((kl + d) % n_kl, ly)
-        dimg[at(pair_slot), :] = image_sum(d).astype(BF16)
-        q = ids["gz"] + d
-        send(piece(dimg, pair_slot), rz.at[d - 1], q, q, dev(k_=kh * n_kl + (kl + d) % n_kl))
+        rng = chunk_rows(pair_slot, h)
+        v = dimg[rng, :].astype(F32)
+        for e in range(1, n_ly):
+            v = v + ry[(e - 1) * n_kl + d, half[h], :].astype(F32)
+        dimg[rng, :] = v.astype(BF16)
+        q = ids["gz"] + d * CHUNKS + h
+        send(chunk(dimg, pair_slot, h), chunk_of(rz, d - 1, h), q, q, dev(k_=kh * n_kl + (kl + d) % n_kl))
+
+    for h in range(CHUNKS):
+        for j in range(n_kh):
+            text_sum(j, h)
+        for d in range(1, n_kl):
+            image_sum(d, h)
+    for h in range(CHUNKS):
+        got_y(0, h)
 
     total = jnp.broadcast_to(jnp.sum(diverge, axis=1, keepdims=True), (8, 128))
     part[kh] = total
@@ -447,7 +497,8 @@
         lax.fori_loop(0, D // HALF, body, 0)
 
     for d in range(1, n_kl):
-        got(rz.at[d - 1], ids["gz"] + d)
+        for h in range(CHUNKS):
+            got(chunk_of(rz, d - 1, h), ids["gz"] + d * CHUNKS + h)
 
     def image_terms(rng):
         o = pl.multiple_of(slot0 * D + rng.start, HALF)
@@ -459,20 +510,21 @@
         return v
     finish(si, image_terms, gi_out)
 
-    for h in range(n_kh):
-        @pl.when(h * n_kl + src_kl != k)
+    for g in range(n_kh):
+        @pl.when(g * n_kl + src_kl != k)
         def _():
-            got(r3.at[h], ids["dz"] + h)
-    finish(st, lambda rng: sum(r3[h, rng, :].astype(F32) for h in range(n_kh)), gt_out)
+            for h in range(CHUNKS):
+                got(chunk_of(r3, g, h), ids["dz"] + g * CHUNKS + h)
+    finish(st, lambda rng: sum(r3[g, rng, :].astype(F32) for g in range(n_kh)), gt_out)
 
     drain()
     for j in range(n_kh):
-        dest = kl * n_kh + j
-        op = copy(piece(dtxt, tslot(j, lx, c)), r3.at[kh], ids["dz"] + j, ids["dz"] + kh, dev(k_=dest))
-
-        @pl.when(dest != k)
-        def _():
-            op.wait_send()
+        for h in range(CHUNKS):
+            dest, op = owner_copy(j, h)
+
+            @pl.when(dest != k)
+            def _():
+                op.wait_send()
 
 
 def on_device(n_row, n_loop, si, st, ti, tt, ssc, tsc):

time: 110 us -> 96.1 us (0.87); the launches traced: 109 us -> 95.9 us
  Pallas kernels: 103 us -> 90.3 us
    pallas_call x1, Pallas kernels: 103 us -> 90.3 us  [on_device(): pl.pallas_call(functools.partial(kernel, dims, ids), out_shape=(jax.Shape...]
where the time goes in v2:
time: 96.1 us; the launch traced here: 95.9 us
  Pallas kernels  90.3 us (94%)
  local copies, waits for them, and re-layouts  3.67 us (4%)
  between operations  1.93 us (2%)
    pallas_call x1, Pallas kernels, on_device(): pl.pallas_call(functools.partial(kernel, dims, ids), out_shape=(jax.Shape...  90.3 us
    unnamed x4, local copies, waits for them, and re-layouts  2.49 us

profile of v2, /device:TPU:21, one launch (start us, length us, event | category | flops | bytes accessed | tf_op | source)
XLA Modules:
  0.0 95.9 jit_solution(12340642193924373124)
XLA Ops:
  1.9 90.3 %shard_map.85 = (f32[8,128]{1,0:T(8,128)}, bf16[160,1024]{1,0:T(8,128)(2,1)}, bf16[160,1024]{1,0:T(8,128)(2,1)}) custom-call(bf16[160,1024]{1,0:T(8,128)(2,1)} %si.1, bf16[160,1024]{1,0:T(8,128)(2,1)} %st.1, bf16[640,256]{1,0:T(8,128)(2,1)} %ti.1, bf16[640,256]{1,0:T(8,128)(2,1)} %tt.1, f32[1]{0:T(128)S(6)} %copy.11.ssc, f32[1]{0:T(128)S(6)} %copy.12.tsc), custom_call_target="tpu_custom_call" | custom-call | tf_op jit(solution)/shard_map/pallas_call | solution.py:541
  92.3 1.2 %slice.3 = f32[1,1]{1,0:T(1,128)} slice(f32[8,128]{1,0:T(8,128)} %get-tuple-element.6), slice={[0:1], [0:1]} | slice | bytes 8 | tf_op jit(solution)/shard_map/slice | solution.py:571
  93.4 0.0 copy-start
  93.4 1.8 %copy.13 = bf16[160,1024]{1,0:T(8,128)(2,1)} copy(bf16[160,1024]{1,0:T(8,128)(2,1)} %get-tuple-element.13) | data formatting | bytes 655360
  95.2 0.0 copy-done
  95.2 0.7 copy.14
Async XLA Ops:
  93.4 1.8 %copy-start = (bf16[160,1024]{1,0:T(8,128)(2,1)S(1)}, bf16[160,1024]{1,0:T(8,128)(2,1)}, u32[]{:S(2)}) copy-start(bf16[160,1024]{1,0:T(8,128)(2,1)} %get-tuple-element.14) | copy-start | bytes 983044

commit v3 on v2

--- a/solution.py
+++ b/solution.py
@@ -143,7 +143,7 @@
         n = jnp.sqrt(n2)
         return n, 1.0 / n
 
-    HALF = 16
+    HALF = Dc if Dc <= 80 else 16
 
     def unit_to(src, dst, base, h):
         def body(i, _):
@@ -235,12 +235,11 @@
                 q = ids[("tc", a)] + (e * n_kh + j) * CHUNKS + h
                 send(chunk(buf, s, h), chunk(buf, s, h), q, q, dev(c_=1 - c))
 
-    def text_finish(a, buf):
-        for h in range(CHUNKS):
-            for e in range(n_lx):
-                for j in range(n_kh):
-                    s = tslot(j, (lx + n_lx - e) % n_lx, 1 - c)
-                    got(chunk(buf, s, h), ids[("tc", a)] + (e * n_kh + j) * CHUNKS + h)
+    def text_finish(a, buf, e):
+        for h in range(CHUNKS):
+            for j in range(n_kh):
+                s = tslot(j, (lx + n_lx - e) % n_lx, 1 - c)
+                got(chunk(buf, s, h), ids[("tc", a)] + (e * n_kh + j) * CHUNKS + h)
 
     def teacher_wait(src, raw, base_id):
         raw[l] = src[at(l), :]
@@ -280,28 +279,35 @@
         text_relay(1, txt_t, h)
         image_relay(1, img_t, h)
     image_finish(0, img_s)
-    text_finish(0, txt_s)
+    for e in range(n_lx):
+        text_finish(0, txt_s, e)
 
     TILE = 2 * D
 
-    def logits(txt, img, scale, out):
-        def body(i, m):
-            o = pl.multiple_of(i * TILE, TILE)
+    def logits(txt, img, scale, out, e, m):
+        def body(j, m):
+            o = pl.multiple_of((j * n_lx + (lx + n_lx - e) % n_lx) * TILE, TILE)
             v = scale * lax.dot_general(
                 txt[pl.ds(o, TILE), :], img[...], (((1,), (1,)), ((), ())),
                 preferred_element_type=F32,
             )
             out[pl.ds(o, TILE), :] = v
             return jnp.maximum(m, jnp.max(v.reshape(TILE // 8, 8, rows), axis=0))
-        m = lax.fori_loop(0, cols // TILE, body, jnp.full((8, rows), -jnp.inf, F32))
-        return jnp.max(m, axis=0, keepdims=True)
-
-    smax = logits(txt_s, img_s, sscale, slog)
+        return lax.fori_loop(0, n_kh, body, m)
+
+    low = jnp.full((8, rows), -jnp.inf, F32)
+    top = low
+    for e in range(n_lx):
+        top = logits(txt_s, img_s, sscale, slog, e, top)
+    smax = jnp.max(top, axis=0, keepdims=True)
     for h in range(CHUNKS):
         text_cross(1, txt_t, h)
     image_finish(1, img_t)
-    text_finish(1, txt_t)
-    tmax = logits(txt_t, img_t, tscale, tlog)
+    top = low
+    for e in range(n_lx):
+        text_finish(1, txt_t, e)
+        top = logits(txt_t, img_t, tscale, tlog, e, top)
+    tmax = jnp.max(top, axis=0, keepdims=True)
 
     def exps(i, carry):
         a, b, x = carry
@@ -381,6 +387,8 @@
         x_ = (lx + e) % n_lx
         to_core(e)
         dtxt_pieces(x_, c)
+        if e == n_lx - 1:
+            to_core(0)
         for h in range(CHUNKS):
             for j in range(n_kh):
                 i = x_ * n_kh + j
@@ -389,6 +397,8 @@
                 dtxt[rng, :] = (dtxt[rng, :].astype(F32) + r1[i, half[h], :].astype(F32)).astype(BF16)
                 q = ids["dx"] + (e * n_kh + j) * CHUNKS + h
                 send(chunk(dtxt, tslot(j, x_, c), h), chunk_of(r2, (e - 1) * n_kh + j, h), q, q, dev(lx_=x_))
+
+    dtxt_pieces(lx, c)
 
     KT = 256
     dimg_acc[...] = jnp.zeros_like(dimg_acc)
@@ -411,8 +421,6 @@
                 q = ids["gy"] + (e * n_kl + d) * CHUNKS + h
                 send(chunk(dimg, islot((kl + d) % n_kl, y_), h), chunk_of(ry, (e - 1) * n_kl + d, h), q, q, dev(ly_=y_))
 
-    to_core(0)
-    dtxt_pieces(lx, c)
 
     def owner_copy(j, h):
         dest = kl * n_kh + j
@@ -484,15 +492,10 @@
     total = part[base] + part[base + 1]
     loss_out[...] = total / float(D * n_row * n_loop)
 
-    def finish(src, terms, out):
+    def add_terms(terms, out):
         def body(i, _):
             rng = pl.ds(pl.multiple_of(i * HALF, HALF), HALF)
-            x = src[rng, :].astype(F32)
-            n, inv = inv_norm(x)
-            u = x * inv
-            g = terms(rng)
-            inner = jnp.sum(g * u, axis=1, keepdims=True)
-            out[rng, :] = ((g - u * inner) * inv).astype(BF16)
+            out[rng, :] = terms(rng)
             return 0
         lax.fori_loop(0, D // HALF, body, 0)
 
@@ -508,14 +511,14 @@
         for d in range(1, n_kl):
             v = v + rz[d - 1, rng, :].astype(F32)
         return v
-    finish(si, image_terms, gi_out)
+    add_terms(image_terms, gi_out)
 
     for g in range(n_kh):
         @pl.when(g * n_kl + src_kl != k)
         def _():
             for h in range(CHUNKS):
                 got(chunk_of(r3, g, h), ids["dz"] + g * CHUNKS + h)
-    finish(st, lambda rng: sum(r3[g, rng, :].astype(F32) for g in range(n_kh)), gt_out)
+    add_terms(lambda rng: sum(r3[g, rng, :].astype(F32) for g in range(n_kh)), gt_out)
 
     drain()
     for j in range(n_kh):
@@ -525,6 +528,23 @@
             @pl.when(dest != k)
             def _():
                 op.wait_send()
+
+
+def back_norms(si, st, total, di, dt, loss_out, gi_out, gt_out):
+    loss_out[0] = total[0, 0]
+    D = si.shape[0]
+    block = 32 if D % 32 == 0 else 16
+
+    def body(i, _):
+        rng = pl.ds(pl.multiple_of(i * block, block), block)
+        for src, grad_unit, out in ((si, di, gi_out), (st, dt, gt_out)):
+            x = src[rng, :].astype(F32)
+            g = grad_unit[rng, :]
+            inv = 1.0 / jnp.sqrt(jnp.sum(x * x, axis=1, keepdims=True) + EPS)
+            along = jnp.sum(g * x, axis=1, keepdims=True) * inv * inv
+            out[rng, :] = ((g - x * along) * inv).astype(BF16)
+        return 0
+    lax.fori_loop(0, D // block, body, 0, unroll=True)
 
 
 def on_device(n_row, n_loop, si, st, ti, tt, ssc, tsc):
@@ -542,8 +562,8 @@
         functools.partial(kernel, dims, ids),
         out_shape=(
             jax.ShapeDtypeStruct((8, 128), F32),
-            jax.ShapeDtypeStruct((D, code), BF16),
-            jax.ShapeDtypeStruct((D, code), BF16),
+            jax.ShapeDtypeStruct((D, code), F32),
+            jax.ShapeDtypeStruct((D, code), F32),
         ),
         in_specs=[vm] * 4 + [sm] * 2,
         out_specs=(vm, vm, vm),
@@ -568,7 +588,16 @@
             collective_id=0, has_side_effects=True, vmem_limit_bytes=67043328,
         ),
     )(si, st, ti, tt, ssc, tsc)
-    return loss[0, :1], gi, gt
+    return pl.pallas_call(
+        back_norms,
+        out_shape=(
+            jax.ShapeDtypeStruct((1,), F32),
+            jax.ShapeDtypeStruct((D, code), BF16),
+            jax.ShapeDtypeStruct((D, code), BF16),
+        ),
+        in_specs=[vm] * 5,
+        out_specs=(sm, vm, vm),
+    )(si, st, loss, gi, gt)
 
 
 def solution(mesh):

time: 96.1 us -> 90.8 us (0.945)
  local copies, waits for them, and re-layouts: 3.67 us -> 0 us
  Pallas kernels: 90.3 us -> 88.7 us
    pallas_call x1, Pallas kernels: 90.3 us -> 85.9 us  [on_device(): pl.pallas_call(functools.partial(kernel, dims, ids), out_shape=(jax.Shape...]
    pallas_call x0 -> x1, Pallas kernels: none -> 2.77 us  [on_device(): pl.pallas_call(back_norms, out_shape=(jax.ShapeDtypeStruct((1,), F32), ja...]
    unnamed x4 -> x0, local copies, waits for them, and re-layouts: 2.49 us -> none
    slice x1 -> x0, local copies, waits for them, and re-layouts: 1.18 us -> none  [on_device(): return (loss[0, :1], gi, gt)]
where the time goes in v3:
time: 90.8 us; the launch traced here: 90.6 us
  Pallas kernels  88.7 us (98%)
  between operations  1.93 us (2%)
    pallas_call x1, Pallas kernels, on_device(): pl.pallas_call(functools.partial(kernel, dims, ids), out_shape=(jax.Shape...  85.9 us
    pallas_call x1, Pallas kernels, on_device(): pl.pallas_call(back_norms, out_shape=(jax.ShapeDtypeStruct((1,), F32), ja...  2.77 us

profile of v3, /device:TPU:21, one launch (start us, length us, event | category | flops | bytes accessed | tf_op | source)
XLA Modules:
  0.0 90.6 jit_solution(14251150806997086170)
XLA Ops:
  1.9 85.9 %shard_map.85 = (f32[8,128]{1,0:T(8,128)}, f32[160,1024]{1,0:T(8,128)}, f32[160,1024]{1,0:T(8,128)}) custom-call(bf16[160,1024]{1,0:T(8,128)(2,1)} %si.3, bf16[160,1024]{1,0:T(8,128)(2,1)} %st.3, bf16[640,256]{1,0:T(8,128)(2,1)} %ti.1, bf16[640,256]{1,0:T(8,128)(2,1)} %tt.1, f32[1]{0:T(128)S(6)} %copy.9.ssc, f32[1]{0:T(128)S(6)} %copy.10.tsc), custom_call_target="tpu_custom_call" | custom-call | tf_op jit(solution)/shard_map/pallas_call | solution.py:561
  87.9 2.8 %shard_map.86 = (f32[1]{0:T(128)}, bf16[160,1024]{1,0:T(8,128)(2,1)}, bf16[160,1024]{1,0:T(8,128)(2,1)}) custom-call(bf16[160,1024]{1,0:T(8,128)(2,1)} %si.3, bf16[160,1024]{1,0:T(8,128)(2,1)} %st.3, f32[8,128]{1,0:T(8,128)} %get-tuple-element.6.total, f32[160,1024]{1,0:T(8,128)} %get-tuple-element.7.di, f32[160,1024]{1,0:T(8,128)} %get-tuple-element.8.dt), custom_call_target="tpu_custom_call" | custom-call | tf_op jit(solution)/shard_map/pallas_call | solution.py:591

commit v4 on v3

--- a/solution.py
+++ b/solution.py
@@ -264,9 +264,9 @@
         unit_to(si, img_s, slot0 * D, h)
         image_first(0, img_s, h)
     for h in range(CHUNKS):
-        text_relay(0, txt_s, h)
-        image_relay(0, img_s, h)
         if h == 0:
+            text_relay(0, txt_s, h)
+            image_relay(0, img_s, h)
             teacher_wait(tt, raw_t, ids["t_txt"])
         teacher_unit(raw_t, own_t, 0, h)
         text_first(1, own_t, txt_t, h)
@@ -274,6 +274,9 @@
             teacher_wait(ti, raw_i, ids["t_img"])
         teacher_unit(raw_i, img_t, slot0 * D, h)
         image_first(1, img_t, h)
+    for h in range(1, CHUNKS):
+        text_relay(0, txt_s, h)
+        image_relay(0, img_s, h)
     for h in range(CHUNKS):
         text_cross(0, txt_s, h)
         text_relay(1, txt_t, h)
@@ -398,8 +401,6 @@
                 q = ids["dx"] + (e * n_kh + j) * CHUNKS + h
                 send(chunk(dtxt, tslot(j, x_, c), h), chunk_of(r2, (e - 1) * n_kh + j, h), q, q, dev(lx_=x_))
 
-    dtxt_pieces(lx, c)
-
     KT = 256
     dimg_acc[...] = jnp.zeros_like(dimg_acc)
 
@@ -421,6 +422,8 @@
                 q = ids["gy"] + (e * n_kl + d) * CHUNKS + h
                 send(chunk(dimg, islot((kl + d) % n_kl, y_), h), chunk_of(ry, (e - 1) * n_kl + d, h), q, q, dev(ly_=y_))
 
+
+    dtxt_pieces(lx, c)
 
     def owner_copy(j, h):
         dest = kl * n_kh + j

time: 90.8 us -> 90.8 us (level)
  no operation moved by 1% of the time
where the time goes in v4:
time: 90.8 us; the launch traced here: 90.6 us
  Pallas kernels  88.7 us (98%)
  between operations  1.93 us (2%)
    pallas_call x1, Pallas kernels, on_device(): pl.pallas_call(functools.partial(kernel, dims, ids), out_shape=(jax.Shape...  85.9 us
    pallas_call x1, Pallas kernels, on_device(): pl.pallas_call(back_norms, out_shape=(jax.ShapeDtypeStruct((1,), F32), ja...  2.77 us

profile of v4, /device:TPU:21, one launch (start us, length us, event | category | flops | bytes accessed | tf_op | source)
XLA Modules:
  0.0 90.6 jit_solution(7098716617414851353)
XLA Ops:
  1.9 85.9 %shard_map.85 = (f32[8,128]{1,0:T(8,128)}, f32[160,1024]{1,0:T(8,128)}, f32[160,1024]{1,0:T(8,128)}) custom-call(bf16[160,1024]{1,0:T(8,128)(2,1)} %si.3, bf16[160,1024]{1,0:T(8,128)(2,1)} %st.3, bf16[640,256]{1,0:T(8,128)(2,1)} %ti.1, bf16[640,256]{1,0:T(8,128)(2,1)} %tt.1, f32[1]{0:T(128)S(6)} %copy.9.ssc, f32[1]{0:T(128)S(6)} %copy.10.tsc), custom_call_target="tpu_custom_call" | custom-call | tf_op jit(solution)/shard_map/pallas_call | solution.py:564
  87.9 2.8 %shard_map.86 = (f32[1]{0:T(128)}, bf16[160,1024]{1,0:T(8,128)(2,1)}, bf16[160,1024]{1,0:T(8,128)(2,1)}) custom-call(bf16[160,1024]{1,0:T(8,128)(2,1)} %si.3, bf16[160,1024]{1,0:T(8,128)(2,1)} %st.3, f32[8,128]{1,0:T(8,128)} %get-tuple-element.6.total, f32[160,1024]{1,0:T(8,128)} %get-tuple-element.7.di, f32[160,1024]{1,0:T(8,128)} %get-tuple-element.8.dt), custom_call_target="tpu_custom_call" | custom-call | tf_op jit(solution)/shard_map/pallas_call | solution.py:594
